TPU v7x, 256 devices: a whole 4x4x8 slice. The times are simulated.
256 devices in a mesh: expert: 8 (over x, core), latent: 32 (over y, z).
Axes of the slice: x: 4, y: 4, z: 8, core: 2. Of those that a mesh axis runs over, the one named last changes fastest.
Arguments:
- tokens: bfloat16 [2048, 2560], P(('expert', 'latent')), may hold values from -6 to 6
- route: int32 [2048, 1], P(('expert', 'latent')), may hold values from 0 to 7; in each aligned block of 8 rows (0 to 7, 8 to 15, ...) at most 2 rows name the same one
- blocks: int32 [2048, 64], P(('expert', 'latent')), may hold values from 0 to 255, all different within a row
- weight: bfloat16 [8, 2560, 32768], P('expert', None, 'latent'), may hold values from -0.125 to 0.125
- enc_bias: float32 [8, 32768], P('expert', 'latent'), may hold values from -3 to 3
- dec_bias: float32 [2560], replicated, may hold values from -3 to 3
Outputs:
- grad_weight: bfloat16 [8, 2560, 32768], P('expert', None, 'latent')
- grad_enc: float32 [8, 32768], P('expert', 'latent')
- grad_dec: float32 [2560], replicated
- loss: float32 [], replicated
Inputs may be any that keep to these rules, and one draw needn't show every extreme that they name: `route`: within the rows of one device (aligned blocks of 8 rows) no expert is named by more than 2 rows. Each row lists 64 different blocks.
All inputs are finite; a program needn't handle non-finite values.
Results may differ from a plain program's by a relative error of at most 0.012.
The roundings to bfloat16 on the way count: a program that leaves them out, or rounds other values in their place, can miss the bound.
Values may be sent and summed in bfloat16 or wider, within the bound.
No kernel may reach another device: no remote copies, remote signals or barrier semaphores. Data moves between devices by JAX's collectives and lax.ppermute only.
A program may use at most 128 MiB of HBM per device.

v0:
```python
import jax
import jax.numpy as jnp
from jax import lax
from jax.sharding import PartitionSpec as P

BLK = 128
CAP = 2


def shards(tokens, route, blocks, weight, enc_bias, dec_bias):
    n_expert = lax.axis_size("expert")
    n_latent = lax.axis_size("latent")
    width = tokens.shape[1]
    list_len = blocks.shape[1]
    expert_of = route[:, 0]
    one_hot = (expert_of[:, None] == jnp.arange(n_expert, dtype=jnp.int32)[None, :]).astype(
        jnp.int32
    )
    earlier = jnp.sum((jnp.cumsum(one_hot, axis=0) - one_hot) * one_hot, axis=1)
    target = expert_of * CAP + earlier
    send_rows = jnp.zeros((n_expert * CAP, width), jnp.bfloat16).at[target].set(tokens)
    send_rows = send_rows.reshape(n_expert, CAP, width)
    send_lists = jnp.full((n_expert * CAP, list_len), -1, jnp.int32).at[target].set(blocks)
    send_lists = send_lists.reshape(n_expert, CAP, list_len)
    got_rows, got_lists = (
        lax.all_to_all(send_rows, "expert", split_axis=0, concat_axis=0, tiled=True),
        lax.all_to_all(send_lists, "expert", split_axis=0, concat_axis=0, tiled=True),
    )
    all_rows, all_lists = (
        lax.all_gather(got_rows[None], "latent", axis=0, tiled=True),
        lax.all_gather(got_lists[None], "latent", axis=0, tiled=True),
    )
    token_rows = all_rows.reshape(-1, width)
    listed = all_lists.reshape(-1, list_len)
    row_count = token_rows.shape[0]
    valid = (listed[:, 0] >= 0).astype(jnp.float32)
    slice_index = lax.axis_index("latent")
    weights_here = weight[0]
    per_slice = weights_here.shape[1] // BLK
    own_blocks = slice_index * per_slice + jnp.arange(per_slice, dtype=jnp.int32)
    chosen = jnp.any(listed[:, :, None] == own_blocks[None, None, :], axis=1).astype(jnp.float32)
    mask = jnp.repeat(chosen, BLK, axis=1)
    rows_f32 = token_rows.astype(jnp.float32)
    shifted = (rows_f32 - dec_bias).astype(jnp.bfloat16)
    pre_act = jnp.dot(shifted, weights_here, preferred_element_type=jnp.float32) + enc_bias[0]
    active = jnp.maximum(pre_act, 0.0) * mask
    active_bf = active.astype(jnp.bfloat16)
    share = row_count // n_latent
    first_row = slice_index * share
    along_width = (((1,), (1,)), ((), ()))
    partial_sum = lax.dot_general(
        active_bf, weights_here, along_width, preferred_element_type=jnp.float32
    )
    summed = lax.psum(partial_sum, "latent")
    error_all = (summed + dec_bias - rows_f32) * valid[:, None]
    error_bf = error_all.astype(jnp.bfloat16)
    error_share = lax.dynamic_slice_in_dim(error_all, first_row, share, 0)
    grad_act = jnp.dot(error_bf, weights_here, preferred_element_type=jnp.float32)
    grad_pre = grad_act * (pre_act > 0.0).astype(jnp.float32) * mask
    grad_pre_bf = grad_pre.astype(jnp.bfloat16)
    along_rows = (((0,), (0,)), ((), ()))
    grad_here = lax.dot_general(
        shifted, grad_pre_bf, along_rows, preferred_element_type=jnp.float32
    )
    grad_here = grad_here + lax.dot_general(
        error_bf, active_bf, along_rows, preferred_element_type=jnp.float32
    )
    grad_bias = jnp.sum(grad_pre, axis=0)
    pulled = jnp.dot(
        weights_here, grad_bias.astype(jnp.bfloat16), preferred_element_type=jnp.float32
    )
    bias_term = jnp.sum(error_share, axis=0) - pulled
    loss_term = 0.5 * jnp.sum(error_share * error_share)
    grad_dec, loss_sum = lax.psum((bias_term, loss_term), ("expert", "latent"))
    loss = loss_sum / (tokens.shape[0] * n_expert * n_latent)
    return (grad_here.astype(jnp.bfloat16)[None], grad_bias[None], grad_dec, loss)


def solution(mesh):
    return jax.shard_map(
        shards,
        mesh=mesh,
        in_specs=(
            P(("expert", "latent"), None),
            P(("expert", "latent"), None),
            P(("expert", "latent"), None),
            P("expert", None, "latent"),
            P("expert", "latent"),
            P(),
        ),
        out_specs=(P("expert", None, "latent"), P("expert", "latent"), P(), P()),
        check_vma=False,
    )
```

profile of v0, /device:TPU:1, one launch (start us, length us, event | category | flops | bytes accessed | tf_op | source)
XLA Modules:
  0.0 402.3 jit_solution(3232776257881222928)
XLA Ops:
  7.2 0.0 all-gather.4.cloned.1.call-start
  7.2 0.7 fusion.24
  8.0 0.8 select_reduce_fusion
  8.8 0.7 fusion.25
  9.5 0.9 scatter_custom_fusion
  10.4 11.2 %all_to_all.10 = bf16[8,2,2560]{2,1,0:T(2,128)(2,1)} all-to-all(bf16[8,2,2560]{2,1,0:T(2,128)(2,1)S(1)} %reshape.33), channel_id=1, replica_groups=mesh['expert'=8,'latent'=32] {'expert'}, dimensions={0} | all-to-all | bytes 163840 | tf_op jit(solution)/shard_map/all_to_all | solution.py:26
  21.6 0.0 all-gather.4.cloned.1.call-update
  21.7 0.8 scatter_custom_fusion.1
  22.4 0.7 reshape.68
  23.1 4.0 all-to-all-start.1
  27.1 4.5 %all-to-all-done.1 = s32[8,1,128]{2,1,0:T(1,128)S(1)} async-done(((s32[8,1,128]{2,1,0:T(1,128)}), s32[8,1,128]{2,1,0:T(1,128)S(1)}, u32[]{:S(2)}, u32[]{:S(2)}) %all-to-all-start.1) | async-done | bytes 4128 | tf_op jit(solution)/shard_map/all_to_all | solution.py:27
  31.6 0.5 broadcast.43
  32.2 0.7 reduce.4
  32.8 0.1 reshape.69
  32.9 40.8 %all-gather.1 = s32[256,2,64]{2,1,0:T(2,128)S(1)} all-gather(s32[8,2,64]{2,1,0:T(2,128)S(1)} %reshape.69), channel_id=3, replica_groups=mesh['expert'=8,'latent'=32] {'latent'}, dimensions={0}, use_global_device_ids=true | all-gather | bytes 135168 | tf_op jit(solution)/shard_map/all_gather | solution.py:31
  73.7 0.1 copy.12
  73.8 0.2 compare_reduce_fusion
  74.1 0.1 copy.13
  74.2 24.0 %all-gather.4.cloned.1.call-done = bf16[256,2,2560]{2,1,0:T(2,128)(2,1)} async-done(((bf16[8,2,2560]{2,1,0:T(2,128)(2,1)}), bf16[256,2,2560]{2,1,0:T(2,128)(2,1)}) %all-gather.4.cloned.1.call-update) | async-done | bytes 2621456 | tf_op jit(solution)/shard_map/all_gather | solution.py:30
  98.1 3.5 convert_element_type.56
  101.7 2.3 subtract_convert_fusion
  104.0 0.0 copy-start.6
  104.0 2.6 convert_element_type.47
  106.6 0.6 broadcast_in_dim.32
  107.2 0.0 copy-start.1
  107.2 0.0 copy-done.6
  107.2 0.0 slice-start.3
  107.3 8.7 %fusion.11 = (bf16[512,1024]{1,0:T(8,128)(2,1)S(1)}, f32[512,1024]{1,0:T(8,128)}) fusion(f32[64,8,8,128]{3,2,1,0:T(8,128)S(1)} %bitcast.51, f32[1024]{0:T(1024)S(1)} %bitcast.57, bf16[512,2560]{1,0:T(8,128)(2,1)} %convert_element_type.47, bf16[1,2560,1024]{2,1,0:T(8,128)(2,1)} %param.9), kind=kOutput, calls=%fused_computation.19 | convolution fusion | flops 2686451712 | bytes 13111296 | tf_op jit(solution)/shard_map/dot_general | solution.py:45
  116.0 1.0 copy-done.3
  117.0 4.7 %fusion.4 = f32[512,2560]{1,0:T(8,128)} fusion(bf16[512,1024]{1,0:T(8,128)(2,1)S(1)} %get-tuple-element.8, bf16[1,2560,1024]{2,1,0:T(8,128)(2,1)S(1)} %bitcast.46), kind=kOutput, calls=%fused_computation.7 | convolution fusion | flops 2684354560 | bytes 11534336 | tf_op jit(solution)/shard_map/dot_general | solution.py:51
  121.7 0.0 all-reduce.3.cloned.1.call-update
  121.7 0.1 convert_reduce_fusion
  121.8 1.6 copy-done
  123.4 2.9 reshape.36
  126.4 168.2 %all-reduce.3.cloned.1.call-done = f32[512,2560]{1,0:T(8,128)} async-done(((f32[512,2560]{1,0:T(8,128)}), f32[512,2560]{1,0:T(8,128)}) %all-reduce.3.cloned.1.call-update) | async-done | bytes 5242896 | tf_op jit(solution)/shard_map/psum | solution.py:54
  294.5 4.9 %subtract_multiply_fusion = f32[512,2560]{1,0:T(8,128)S(1)} fusion(f32[512,2560]{1,0:T(8,128)} %reshape.36, f32[512,2560]{1,0:T(8,128)} %all-reduce.3.cloned.1.call-done, f32[512]{0:T(512)S(1)} %convert_reduce_fusion, f32[2560]{0:T(1024)S(1)} %copy-done.4), kind=kLoop, calls=%fused_computation.11 | loop fusion | flops 3932160 | bytes 15740928 | tf_op jit(solution)/shard_map/mul | solution.py:55
  299.5 0.0 slice-start.1
  299.5 5.9 %fusion.26 = (f32[1024]{0:T(1024)S(1)}, bf16[512,1024]{1,0:T(8,128)(2,1)S(1)}) fusion(f32[64,8,8,128]{3,2,1,0:T(8,128)S(1)} %bitcast.52, bf16[1,2560,1024]{2,1,0:T(8,128)(2,1)} %param.9, f32[512,2560]{1,0:T(8,128)S(1)} %subtract_multiply_fusion, f32[512,1024]{1,0:T(8,128)S(1)} %copy-done.7, f32[1024]{0:T(1024)S(1)} %bitcast.58), kind=kOutput, calls=%fused_computation.40 | convolution fusion | flops 2688809984 | bytes 15736832 | tf_op jit(solution)/shard_map/dot_general | solution.py:58
  305.4 0.0 copy-start.5
  305.4 0.0 slice-done
  305.4 0.0 slice-done.1
  305.4 0.0 slice-start.4
  305.5 3.0 fusion.9
  308.5 0.0 slice-start.5
  308.5 6.5 %fusion.8 = bf16[1,2560,1024]{2,1,0:T(8,128)(2,1)} fusion(f32[2560,1024]{1,0:T(8,128)S(1)} %fusion.9, bf16[512,1024]{1,0:T(8,128)(2,1)} %copy-done.3, f32[512,2560]{1,0:T(8,128)S(1)} %subtract_multiply_fusion), kind=kOutput, calls=%fused_computation.14 | convolution fusion | flops 2690908160 | bytes 22020096 | tf_op jit(solution)/shard_map/dot_general | solution.py:65
  315.0 0.6 multiply_reduce_fusion
  315.6 1.5 fusion.16
  317.8 75.9 %all-reduce = (f32[2560]{0:T(1024)}, f32[]{:T(128)}) all-reduce(f32[2560]{0:T(1024)S(1)} %sub.28, f32[]{:T(128)S(6)} %mul_shard_map.3), channel_id=1, replica_groups=mesh['expert'=8,'latent'=32] {'expert','latent'}, use_global_device_ids=true, to_apply=%region_8.9 | all-reduce | flops 2561 | bytes 20488 | tf_op jit(solution)/shard_map/psum | solution.py:74
  (27 shorter events, 0.1 us)
Async XLA Ops:
  7.2 94.5 %copy-start.4 = (f32[2560]{0:T(1024)S(1)}, f32[2560]{0:T(1024)}, u32[]{:S(2)}) copy-start(f32[2560]{0:T(1024)} %param.11) | copy-start | bytes 30724
  7.2 91.0 %all-gather.4.cloned.1.call-start = ((), (), s32[]{:S(2)}) async-start(), calls=%async_computation.3 | async-start | bytes 2703360 | tf_op jit(solution)/shard_map/all_gather | solution.py:30
  23.1 8.5 %all-to-all-start.1 = ((s32[8,1,128]{2,1,0:T(1,128)}), s32[8,1,128]{2,1,0:T(1,128)S(1)}, u32[]{:S(2)}, u32[]{:S(2)}) async-start(s32[8,1,128]{2,1,0:T(1,128)} %reshape.68), calls=%async_computation.1 | async-start | bytes 8192 | tf_op jit(solution)/shard_map/all_to_all | solution.py:27
  27.1 267.4 %all-reduce.3.cloned.1.call-start = ((), (), s32[]{:S(2)}) async-start(), calls=%async_computation.2 | async-start | bytes 10485760 | tf_op jit(solution)/shard_map/psum | solution.py:54
  104.0 3.2 copy-start.6
  106.6 10.4 %slice-start.2 = ((s8[5242880]{0:T(1024)(128)(4,1)}), s8[4194304]{0:T(1024)(128)(4,1)S(1)}, s32[]{:S(2)}) async-start(s8[5242880]{0:T(1024)(128)(4,1)} %bitcast.45), calls=%async_computation.6 | async-start | bytes 8388608
  107.2 8.8 %copy-start.1 = (f32[512,8,128]{2,1,0:T(8,128)}, f32[512,8,128]{2,1,0:T(8,128)S(1)}, u32[]{:S(2)}) copy-start(f32[512,8,128]{2,1,0:T(8,128)S(1)} %broadcast_in_dim.32) | copy-start | bytes 6291460
  107.2 9.7 %slice-start.3 = ((s8[5242880]{0:T(1024)(128)(4,1)}), s8[1048576]{0:T(1024)(128)(4,1)S(1)}, s32[]{:S(2)}) async-start(s8[5242880]{0:T(1024)(128)(4,1)} %bitcast.45), calls=%async_computation.7 | async-start | bytes 2097152
  116.0 1.0 copy-start.3
  121.7 1.7 copy-start
  126.3 173.1 %copy-start.2 = (f32[512,8,128]{2,1,0:T(8,128)S(1)}, f32[512,8,128]{2,1,0:T(8,128)}, u32[]{:S(2)}) copy-start(f32[512,8,128]{2,1,0:T(8,128)} %copy-done.1) | copy-start | bytes 6291460
  294.5 4.9 %copy-start.7 = (f32[512,1024]{1,0:T(8,128)S(1)}, f32[512,1024]{1,0:T(8,128)}, u32[]{:S(2)}) copy-start(f32[512,1024]{1,0:T(8,128)} %get-tuple-element.9) | copy-start | bytes 6291460
  294.5 10.9 %slice-start = ((s8[5242880]{0:T(1024)(128)(4,1)}), s8[1048576]{0:T(1024)(128)(4,1)S(1)}, s32[]{:S(2)}) async-start(s8[5242880]{0:T(1024)(128)(4,1)} %bitcast.42), calls=%async_computation.4 | async-start | bytes 2097152
  299.5 6.0 %slice-start.1 = ((s8[5242880]{0:T(1024)(128)(4,1)}), s8[4194304]{0:T(1024)(128)(4,1)S(1)}, s32[]{:S(2)}) async-start(s8[5242880]{0:T(1024)(128)(4,1)} %bitcast.42), calls=%async_computation.5 | async-start | bytes 8388608
  305.4 10.2 %copy-start.5 = (f32[1024]{0:T(1024)}, f32[1024]{0:T(1024)S(1)}, u32[]{:S(2)}) copy-start(f32[1024]{0:T(1024)S(1)} %get-tuple-element.10) | copy-start | bytes 12292
  305.4 10.2 %slice-start.4 = ((s8[5242880]{0:T(1024)(128)(4,1)}), s8[4194304]{0:T(1024)(128)(4,1)S(1)}, s32[]{:S(2)}) async-start(s8[5242880]{0:T(1024)(128)(4,1)} %bitcast.47), calls=%async_computation.8 | async-start | bytes 8388608
  308.5 7.2 %slice-start.5 = ((s8[5242880]{0:T(1024)(128)(4,1)}), s8[1048576]{0:T(1024)(128)(4,1)S(1)}, s32[]{:S(2)}) async-start(s8[5242880]{0:T(1024)(128)(4,1)} %bitcast.47), calls=%async_computation.9 | async-start | bytes 2097152
Sparse Core Ops, SparseCore 0:
  21.8 76.3 all-gather.3
  121.8 172.6 all-reduce.2
where the time goes:
time: 403 us; the launch traced here: 402 us
  waiting for transfers between devices  197 us (49%)
  blocking collectives  128 us (32%)
  matrix products  30.3 us (8%)
  between operations  16.7 us (4%)
  other arithmetic  14.6 us (4%)
  local copies, waits for them, and re-layouts  12 us (3%)
  starting transfers between devices  4.05 us (1%)
    psum x1, waiting for transfers between devices, shards(): summed = lax.psum(partial_sum, 'latent')  168 us
    psum x1, blocking collectives, shards(): grad_dec, loss_sum = lax.psum((bias_term, loss_term), ('expert', 'latent'))  75.9 us
    all_gather x1, blocking collectives, shards(): lax.all_gather(got_lists[None], 'latent', axis=0, tiled=True)  40.8 us
    all_gather x1, waiting for transfers between devices, shards(): lax.all_gather(got_rows[None], 'latent', axis=0, tiled=True)  24 us
    all_to_all x1, blocking collectives, shards(): lax.all_to_all(send_rows, 'expert', split_axis=0, concat_axis=0, tiled=True)  11.2 us
    dot_general x1, matrix products, shards(): jnp.dot(shifted, weights_here, preferred_element_type=jnp.float32)  8.73 us
  transfers between devices with their start and end apart: 3, of which 3 were waited for; matrix products, arithmetic and copies ran while one was open for 2% of the time, Pallas kernels for 0%

commit v1 on v0

--- a/solution.py
+++ b/solution.py
@@ -5,6 +5,15 @@
 
 BLK = 128
 CAP = 2
+
+
+def advance_the_goods(tile_in):
+    how_many = lax.axis_size("latent")
+    v_now = tile_in
+    for t in [[(k, k ^ m) for k in range(how_many)] for m in (1, 2, 4, 8, 16) if m < how_many]:
+        taken_in = lax.ppermute(v_now, "latent", t)
+        v_now = v_now + taken_in
+    return v_now
 
 
 def shards(tokens, route, blocks, weight, enc_bias, dec_bias):
@@ -51,7 +60,7 @@
     partial_sum = lax.dot_general(
         active_bf, weights_here, along_width, preferred_element_type=jnp.float32
     )
-    summed = lax.psum(partial_sum, "latent")
+    summed = advance_the_goods(partial_sum)
     error_all = (summed + dec_bias - rows_f32) * valid[:, None]
     error_bf = error_all.astype(jnp.bfloat16)
     error_share = lax.dynamic_slice_in_dim(error_all, first_row, share, 0)

time: 403 us -> 1040 us (2.58)
  waiting for transfers between devices: 197 us -> 819 us
    ppermute x0 -> x5, waiting for transfers between devices: none -> 791 us  [advance_the_goods(): taken_in = lax.ppermute(v_now, 'latent', t)]
    psum x1 -> x0, waiting for transfers between devices: 168 us -> none  [shards(): summed = lax.psum(partial_sum, 'latent')]
  transfers between devices with their start and end apart: 3 -> 7, of which waited for: 3 -> 7; matrix products, arithmetic and copies ran while one was open for 2% -> 1% of each run, Pallas kernels for 0% -> 0%
where the time goes in v1:
time: 1040 us
  waiting for transfers between devices  819 us (79%)
  blocking collectives  127 us (12%)
  matrix products  31.8 us (3%)
  other arithmetic  23.3 us (2%)
  between operations  16.8 us (2%)
    ppermute x5, waiting for transfers between devices, advance_the_goods(): taken_in = lax.ppermute(v_now, 'latent', t)  791 us
    psum x1, blocking collectives, shards(): grad_dec, loss_sum = lax.psum((bias_term, loss_term), ('expert', 'latent'))  75.2 us
    all_gather x1, blocking collectives, shards(): lax.all_gather(got_lists[None], 'latent', axis=0, tiled=True)  40.8 us
    all_gather x1, waiting for transfers between devices, shards(): lax.all_gather(got_rows[None], 'latent', axis=0, tiled=True)  24 us
  transfers between devices with their start and end apart: 7, of which 7 were waited for; matrix products, arithmetic and copies ran while one was open for 1% of the time, Pallas kernels for 0%

profile of v1, /device:TPU:1, one launch (start us, length us, event | category | flops | bytes accessed | tf_op | source)
XLA Modules:
  0.0 1036.1 jit_solution(13250028458520086978)
XLA Ops:
  7.2 0.0 all-gather.4.cloned.1.call-start
  7.2 0.7 fusion.24
  8.0 0.8 select_reduce_fusion
  8.8 0.7 fusion.25
  9.5 0.9 scatter_custom_fusion
  10.4 11.2 %all_to_all.10 = bf16[8,2,2560]{2,1,0:T(2,128)(2,1)} all-to-all(bf16[8,2,2560]{2,1,0:T(2,128)(2,1)S(1)} %reshape.33), channel_id=1, replica_groups=mesh['expert'=8,'latent'=32] {'expert'}, dimensions={0} | all-to-all | bytes 163840 | tf_op jit(solution)/shard_map/all_to_all | solution.py:35
  21.6 0.0 all-gather.4.cloned.1.call-update
  21.7 0.8 scatter_custom_fusion.1
  22.4 0.7 reshape.68
  23.1 4.0 all-to-all-start.1
  27.1 4.5 all-to-all-done.1
  31.6 0.5 broadcast.43
  32.2 0.7 reduce.4
  32.8 0.1 reshape.69
  32.9 40.8 %all-gather.1 = s32[256,2,64]{2,1,0:T(2,128)S(1)} all-gather(s32[8,2,64]{2,1,0:T(2,128)S(1)} %reshape.69), channel_id=3, replica_groups=mesh['expert'=8,'latent'=32] {'latent'}, dimensions={0}, use_global_device_ids=true | all-gather | bytes 135168 | tf_op jit(solution)/shard_map/all_gather | solution.py:40
  73.7 0.1 copy.12
  73.8 0.2 compare_reduce_fusion
  74.1 0.1 copy.13
  74.2 24.0 %all-gather.4.cloned.1.call-done = bf16[256,2,2560]{2,1,0:T(2,128)(2,1)} async-done(((bf16[8,2,2560]{2,1,0:T(2,128)(2,1)}), bf16[256,2,2560]{2,1,0:T(2,128)(2,1)}) %all-gather.4.cloned.1.call-update) | async-done | bytes 2621456 | tf_op jit(solution)/shard_map/all_gather | solution.py:39
  98.1 3.5 convert_element_type.56
  101.7 2.3 subtract_convert_fusion
  104.0 2.4 convert_element_type.47
  106.4 0.6 broadcast_in_dim.32
  107.1 0.0 slice-start.1
  107.1 8.7 fusion.11
  115.8 2.9 fusion.4
  118.8 0.6 collective-permute-start
  119.4 110.1 %collective-permute-done = f32[512,2560]{1,0:T(8,128)S(1)} collective-permute-done((f32[512,2560]{1,0:T(8,128)S(1)}, f32[512,2560]{1,0:T(8,128)S(1)}, u32[]{:S(2)}, u32[]{:S(2)}) %collective-permute-start) | collective-permute-done | bytes 5242912 | tf_op jit(solution)/shard_map/ppermute | solution.py:14
  229.5 0.9 add.67
  230.4 1.0 collective-permute-start.1
  231.5 226.4 %collective-permute-done.1 = f32[512,2560]{1,0:T(8,128)S(1)} collective-permute-done((f32[512,2560]{1,0:T(8,128)S(1)}, f32[512,2560]{1,0:T(8,128)S(1)}, u32[]{:S(2)}, u32[]{:S(2)}) %collective-permute-start.1) | collective-permute-done | bytes 5242912 | tf_op jit(solution)/shard_map/ppermute | solution.py:14
  457.9 0.9 add.68
  458.8 2.8 collective-permute-start.2
  461.6 228.1 %collective-permute-done.2 = f32[512,2560]{1,0:T(8,128)S(1)} collective-permute-done((f32[512,2560]{1,0:T(8,128)S(1)}, f32[512,2560]{1,0:T(8,128)S(1)}, u32[]{:S(2)}, u32[]{:S(2)}) %collective-permute-start.2) | collective-permute-done | bytes 5242912 | tf_op jit(solution)/shard_map/ppermute | solution.py:14
  689.7 0.9 add.69
  690.7 0.1 collective-permute-start.3
  690.8 114.1 %collective-permute-done.3 = f32[512,2560]{1,0:T(8,128)S(1)} collective-permute-done((f32[512,2560]{1,0:T(8,128)S(1)}, f32[512,2560]{1,0:T(8,128)S(1)}, u32[]{:S(2)}, u32[]{:S(2)}) %collective-permute-start.3) | collective-permute-done | bytes 5242912 | tf_op jit(solution)/shard_map/ppermute | solution.py:14
  804.9 3.3 add.70
  808.1 0.1 convert_reduce_fusion
  808.3 2.9 reshape.36
  811.2 112.0 %collective-permute-done.4 = f32[512,2560]{1,0:T(8,128)} collective-permute-done((f32[512,2560]{1,0:T(8,128)}, f32[512,2560]{1,0:T(8,128)}, u32[]{:S(2)}, u32[]{:S(2)}) %collective-permute-start.4) | collective-permute-done | bytes 5242912 | tf_op jit(solution)/shard_map/ppermute | solution.py:14
  923.2 7.5 subtract_multiply_fusion
  930.7 5.8 fusion.26
  936.6 5.6 fusion.9
  942.2 7.3 fusion.8
  949.4 0.6 multiply_reduce_fusion
  950.1 1.5 fusion.16
  952.3 75.2 %all-reduce = (f32[2560]{0:T(1024)}, f32[]{:T(128)}) all-reduce(f32[2560]{0:T(1024)S(1)} %sub.28, f32[]{:T(128)S(6)} %mul_shard_map.3), channel_id=1, replica_groups=mesh['expert'=8,'latent'=32] {'expert','latent'}, use_global_device_ids=true, to_apply=%region_7.8 | all-reduce | flops 2561 | bytes 20488 | tf_op jit(solution)/shard_map/psum | solution.py:83
  (37 shorter events, 0.2 us)
Async XLA Ops:
  7.2 94.5 %copy-start.6 = (f32[2560]{0:T(1024)S(1)}, f32[2560]{0:T(1024)}, u32[]{:S(2)}) copy-start(f32[2560]{0:T(1024)} %param.11) | copy-start | bytes 30724
  7.2 91.0 %all-gather.4.cloned.1.call-start = ((), (), s32[]{:S(2)}) async-start(), calls=%async_computation.2 | async-start | bytes 2703360 | tf_op jit(solution)/shard_map/all_gather | solution.py:39
  23.1 8.5 all-to-all-start.1
  104.0 3.1 copy-start.8
  106.4 9.4 slice-start
  107.0 8.8 copy-start.2
  107.1 8.8 slice-start.1
  115.8 3.0 copy-start.4
  118.8 110.7 %collective-permute-start = (f32[512,2560]{1,0:T(8,128)S(1)}, f32[512,2560]{1,0:T(8,128)S(1)}, u32[]{:S(2)}, u32[]{:S(2)}) collective-permute-start(f32[512,2560]{1,0:T(8,128)S(1)} %fusion.4), channel_id=1, source_target_pairs={{0,1},{1,0},{2,3},{3,2},{4,5},{5,4},{6,7},{7,6},{8,9},{9,8},{10,11... | collective-permute-start | bytes 15728648 | tf_op jit(solution)/shard_map/ppermute | solution.py:14
  230.4 227.4 %collective-permute-start.1 = (f32[512,2560]{1,0:T(8,128)S(1)}, f32[512,2560]{1,0:T(8,128)S(1)}, u32[]{:S(2)}, u32[]{:S(2)}) collective-permute-start(f32[512,2560]{1,0:T(8,128)S(1)} %add.67), channel_id=1, source_target_pairs={{0,2},{1,3},{2,0},{3,1},{4,6},{5,7},{6,4},{7,5},{8,10},{9,11},{10,... | collective-permute-start | bytes 15728648 | tf_op jit(solution)/shard_map/ppermute | solution.py:14
  458.8 230.9 %collective-permute-start.2 = (f32[512,2560]{1,0:T(8,128)S(1)}, f32[512,2560]{1,0:T(8,128)S(1)}, u32[]{:S(2)}, u32[]{:S(2)}) collective-permute-start(f32[512,2560]{1,0:T(8,128)S(1)} %add.68), channel_id=1, source_target_pairs={{0,4},{1,5},{2,6},{3,7},{4,0},{5,1},{6,2},{7,3},{8,12},{9,13},{10,... | collective-permute-start | bytes 15728648 | tf_op jit(solution)/shard_map/ppermute | solution.py:14
  690.7 117.6 %copy-start.1 = (bf16[256,2,2560]{2,1,0:T(2,128)(2,1)S(1)}, bf16[256,2,2560]{2,1,0:T(2,128)(2,1)}, u32[]{:S(2)}) copy-start(bf16[256,2,2560]{2,1,0:T(2,128)(2,1)} %all-gather.4.cloned.1.call-done) | copy-start | bytes 7864324
  690.7 114.2 %collective-permute-start.3 = (f32[512,2560]{1,0:T(8,128)S(1)}, f32[512,2560]{1,0:T(8,128)S(1)}, u32[]{:S(2)}, u32[]{:S(2)}) collective-permute-start(f32[512,2560]{1,0:T(8,128)S(1)} %add.69), channel_id=1, source_target_pairs={{0,8},{1,9},{2,10},{3,11},{4,12},{5,13},{6,14},{7,15},{8,0},{9,1},... | collective-permute-start | bytes 15728648 | tf_op jit(solution)/shard_map/ppermute | solution.py:14
  808.1 115.0 %collective-permute-start.4 = (f32[512,2560]{1,0:T(8,128)}, f32[512,2560]{1,0:T(8,128)}, u32[]{:S(2)}, u32[]{:S(2)}) collective-permute-start(f32[512,2560]{1,0:T(8,128)} %add.70), channel_id=1, source_target_pairs={{0,16},{1,17},{2,18},{3,19},{4,20},{5,21},{6,22},{7,23},{8,24},{9,... | collective-permute-start | bytes 15728648 | tf_op jit(solution)/shard_map/ppermute | solution.py:14
  811.2 119.4 %copy-start.3 = (f32[512,8,128]{2,1,0:T(8,128)S(1)}, f32[512,8,128]{2,1,0:T(8,128)}, u32[]{:S(2)}) copy-start(f32[512,8,128]{2,1,0:T(8,128)} %copy-done.2) | copy-start | bytes 6291460
  811.2 119.4 %copy-start.9 = (f32[512,1024]{1,0:T(8,128)S(1)}, f32[512,1024]{1,0:T(8,128)}, u32[]{:S(2)}) copy-start(f32[512,1024]{1,0:T(8,128)} %get-tuple-element.9) | copy-start | bytes 6291460
  930.7 5.9 copy-start
  936.5 13.6 %copy-start.7 = (f32[1024]{0:T(1024)}, f32[1024]{0:T(1024)S(1)}, u32[]{:S(2)}) copy-start(f32[1024]{0:T(1024)S(1)} %get-tuple-element.10) | copy-start | bytes 12292
  936.5 5.6 copy-start.5
  936.5 13.5 %slice-start.2 = ((s8[5242880]{0:T(1024)(128)(4,1)}), s8[4194304]{0:T(1024)(128)(4,1)S(1)}, s32[]{:S(2)}) async-start(s8[5242880]{0:T(1024)(128)(4,1)} %bitcast.45), calls=%async_computation.5 | async-start | bytes 8388608
  942.2 7.9 slice-start.3
Sparse Core Ops, SparseCore 0:
  21.8 76.3 all-gather.3
